TPU v7x, 256 devices: a whole 4x4x8 slice. The times are simulated.
256 devices in a mesh: rows: 64 (over x_hi, y, z), grp: 4 (over x_lo, core).
Axes of the slice: x: 4 (x_hi: 2, x_lo: 2; x = x_hi * 2 + x_lo), y: 4, z: 8, core: 2. Of those that a mesh axis runs over, the one named last changes fastest.
Arguments:
- table: float32 [524288, 256], P(('rows', 'grp')), may hold values from -1.5 to 1.5
- hot_slot: int32 [4096], P(('rows', 'grp')), may hold values from 0 to 2047, as said below
- cold_row: int32 [256, 256, 8], P(('rows', 'grp')), may hold values from 0 to 2047, as said below
- cold_bag: int32 [256, 256, 8], P(('rows', 'grp')), may hold values from 0 to 511
- hot_pick: int32 [65536, 8], P(('rows', 'grp')), may hold values from 0 to 4095
- dense: float32 [65536, 256], P(('rows', 'grp')), may hold values from -6 to 6
- label: int32 [65536], P(('rows', 'grp')), may hold values 0 or 1
Outputs:
- pooled: float32 [65536, 256], P(('rows', 'grp'))
- new_table: float32 [524288, 256], P(('rows', 'grp'))
- hot_new: float32 [4096, 256], replicated
Inputs may be any that keep to these rules, and one draw needn't show every extreme that they name: `hot_slot`: distinct within each device's block of 16 entries; hot row h lies in the shard of device h // 16. `cold_row`: a cold slot never names a hot row of its owner. `cold_bag`: a value of 256 or more marks an empty slot.
All inputs are finite; a program needn't handle non-finite values. No bound on the sum of `label` on one device may be relied on, other than what follows from the above.
Results may differ from a plain program's by a relative error of at most 0.0029.
Values may be sent and summed in bfloat16 or wider, within the bound.
A program may use at most 64 MiB of HBM per device.

v0:
```python
import jax
import jax.numpy as jnp
from jax import lax
from jax.sharding import PartitionSpec as P


def split_up(value, dim, peers):
    shape = value.shape
    blocks = value.reshape(*shape[:dim], peers, shape[dim] // peers, *shape[dim + 1 :])
    return jnp.moveaxis(blocks, dim, 0)


def laid_out(blocks, dim):
    blocks = jnp.moveaxis(blocks, 0, dim)
    shape = blocks.shape
    return blocks.reshape(*shape[:dim], shape[dim] * shape[dim + 1], *shape[dim + 2 :])


def exchange_both(value, axis, axes, splits, concats):
    sizes = [lax.axis_size(a) for a in axes]
    blocks = split_up(value, splits[0], sizes[0])
    blocks = jnp.moveaxis(split_up(blocks, splits[1] + 1, sizes[1]), 0, 1)
    inside = blocks.shape[2:]
    blocks = blocks.reshape(-1, *inside)
    blocks = lax.all_to_all(blocks, axis, split_axis=0, concat_axis=0, tiled=True)
    blocks = laid_out(blocks.reshape(*sizes, *inside), concats[0] + 1)
    return laid_out(blocks, concats[1])


def body(table, hot_slot, cold_row, cold_bag, hot_pick, dense, label):
    n_rows = lax.axis_size("rows")
    n_grp = lax.axis_size("grp")
    width = table.shape[1]
    samples = dense.shape[0]
    own_hot = hot_slot.shape[0]
    slots = cold_row.shape[1] * cold_row.shape[2]
    per_peer = cold_row.shape[2]
    rounded = table.astype(jnp.bfloat16)
    hot_full = lax.all_gather(table[hot_slot], ("rows", "grp"), axis=0, tiled=True)
    hot_copy = hot_full.astype(jnp.bfloat16)
    requests = cold_row[0].reshape(n_rows, n_grp, per_peer)
    arrived = exchange_both(requests, ("rows", "grp"), ("rows", "grp"), (0, 1), (0, 1))
    looked = rounded[arrived.reshape(-1)].reshape(n_rows, n_grp, per_peer, width)
    returned = lax.all_to_all(
        lax.all_to_all(looked, "rows", split_axis=0, concat_axis=0, tiled=True),
        "grp",
        split_axis=1,
        concat_axis=1,
        tiled=True,
    )
    flat_rows = returned.reshape(slots, width)
    bags = cold_bag[0].reshape(slots)
    selector = jnp.arange(samples, dtype=jnp.int32)[:, None] == bags[None, :]
    cold_pooled = jnp.dot(
        selector.astype(jnp.bfloat16), flat_rows, preferred_element_type=jnp.float32
    )
    hot_pooled = jnp.sum(hot_copy[hot_pick].astype(jnp.float32), axis=1)
    pooled = cold_pooled + hot_pooled
    score = jnp.sum(pooled * dense, axis=1) / width**0.5
    err = jax.nn.sigmoid(score) - label.astype(jnp.float32)
    grad = err[:, None] * dense
    slot_grad = lax.dot_general(
        selector.astype(jnp.float32),
        grad,
        (((0,), (0,)), ((), ())),
        precision=lax.Precision.HIGHEST,
        preferred_element_type=jnp.float32,
    )
    delivered = exchange_both(
        slot_grad.reshape(n_rows, n_grp, per_peer, width),
        ("rows", "grp"),
        ("rows", "grp"),
        (0, 1),
        (0, 1),
    )
    table_grad = jax.ops.segment_sum(
        delivered.reshape(slots, width), arrived.reshape(slots), num_segments=table.shape[0]
    )
    hot_total = hot_copy.shape[0]
    spread = jnp.repeat(grad, hot_pick.shape[1], axis=0)
    hot_local = jax.ops.segment_sum(spread, hot_pick.reshape(-1), num_segments=hot_total)
    summed = lax.psum(hot_local, ("rows", "grp"))
    start = lax.axis_index(("rows", "grp")) * own_hot
    own_grad = lax.dynamic_slice_in_dim(summed, start, own_hot, 0)
    table_grad = table_grad.at[hot_slot].add(own_grad)
    new_table = table - 0.1 * table_grad
    hot_new = hot_full - 0.1 * summed
    return (pooled, new_table, hot_new)


def solution(mesh):
    placed = (
        P(("rows", "grp"), None),
        P(("rows", "grp")),
        P(("rows", "grp"), None, None),
        P(("rows", "grp"), None, None),
        P(("rows", "grp"), None),
        P(("rows", "grp"), None),
        P(("rows", "grp")),
    )
    return jax.shard_map(
        body,
        mesh=mesh,
        in_specs=placed,
        out_specs=(P(("rows", "grp"), None), P(("rows", "grp"), None), P()),
        check_vma=False,
    )
```

profile of v0, /device:TPU:2, one launch (start us, length us, event | category | flops | bytes accessed | tf_op | source)
XLA Modules:
  0.0 783.1 jit_solution(3402326476514333365)
XLA Ops:
  7.2 0.0 all-gather.3.cloned.1.call-start
  7.2 0.7 compare_select_fusion.2
  7.9 0.0 copy-start.6
  7.9 0.5 copy-done.6
  8.4 2.8 gather_fusion.1
  11.2 0.0 all-gather.3.cloned.1.call-update
  11.2 1.5 copy.38
  12.7 14.7 %all-to-all-start = ((s32[256,1,1,8]{3,2,1,0:T(1,128)}), s32[256,1,1,8]{3,2,1,0:T(1,128)S(1)}, u32[]{:S(2)}, u32[]{:S(2)}) async-start(s32[256,1,1,8]{3,2,1,0:T(1,128)} %bitcast), calls=%async_computation | async-start | bytes 262144 | tf_op jit(solution)/shard_map/all_to_all | solution.py:25
  27.4 1.7 convert_element_type.14
  29.1 10.6 %all-to-all-done = s32[256,1,1,8]{3,2,1,0:T(1,128)S(1)} async-done(((s32[256,1,1,8]{3,2,1,0:T(1,128)}), s32[256,1,1,8]{3,2,1,0:T(1,128)S(1)}, u32[]{:S(2)}, u32[]{:S(2)}) %all-to-all-start) | async-done | bytes 8224 | tf_op jit(solution)/shard_map/all_to_all | solution.py:25
  39.6 0.2 reshape_reshape.6
  39.8 7.5 gather_fusion
  47.3 34.3 %all_to_all.20 = bf16[64,4,8,256]{3,2,1,0:T(8,128)(2,1)S(1)} all-to-all(bf16[64,4,8,256]{3,2,1,0:T(8,128)(2,1)S(1)} %bitcast.38), channel_id=1, replica_groups=mesh['rows'=64,'grp'=4] {'rows'}, dimensions={0} | all-to-all | bytes 2097152 | tf_op jit(solution)/shard_map/all_to_all | solution.py:45
  81.6 0.0 copy-start.1
  81.6 0.0 copy-start.2
  81.6 0.0 copy-start.4
  81.6 1.0 copy.39
  82.6 4.7 all-to-all-start.2
  87.3 0.0 copy-done.1
  87.3 0.8 copy.43
  88.2 0.0 copy-done.2
  88.2 0.1 copy.41
  88.3 0.1 reshape.82
  88.4 0.0 copy-done.4
  88.4 0.1 copy.37
  88.6 0.1 eq.16
  88.7 12.2 %all-to-all-done.2 = bf16[64,4,8,256]{3,2,0,1:T(8,128)(2,1)S(1)} async-done(((bf16[64,4,8,256]{3,2,0,1:T(8,128)(2,1)}), bf16[64,4,8,256]{3,2,0,1:T(8,128)(2,1)S(1)}, u32[]{:S(2)}, u32[]{:S(2)}) %all-to-all-start.2) | async-done | bytes 1048608 | tf_op jit(solution)/shard_map/all_to_all | solution.py:44
  100.9 1.1 copy.40
  102.0 330.1 %all-gather.3.cloned.1.call-done = f32[4096,256]{1,0:T(8,128)} async-done(((f32[16,256]{1,0:T(8,128)}), f32[4096,256]{1,0:T(8,128)}) %all-gather.3.cloned.1.call-update) | async-done | bytes 4194320 | tf_op jit(solution)/shard_map/all_gather | solution.py:39
  432.1 2.4 convert_element_type.15
  434.5 7.5 gather_fusion.2
  442.0 0.0 copy-start.5
  442.0 0.7 convert_reduce_fusion
  442.7 0.1 copy.42
  442.9 2.0 multiply_reduce_fusion
  444.9 0.0 copy-done.5
  444.9 0.1 broadcast_multiply_fusion
  445.0 3.2 fusion.7
  448.2 0.0 copy-start.3
  448.2 9.4 %all-to-all-start.3 = ((f32[256,1,1,8,256]{4,3,2,1,0:T(8,128)}), f32[256,1,1,8,256]{4,3,2,1,0:T(8,128)S(1)}, u32[]{:S(2)}, u32[]{:S(2)}) async-start(f32[256,1,1,8,256]{4,3,2,1,0:T(8,128)} %fusion.7), calls=%async_computation.3 | async-start | bytes 4194304 | tf_op jit(solution)/shard_map/all_to_all | solution.py:25
  457.5 0.2 all-reduce.2.cloned.1.call-start
  457.7 0.0 copy-done.3
  457.8 0.1 copy.45
  457.9 0.1 reshape.98
  458.0 13.8 %scatter_custom_fusion.1 = f32[4096,256]{1,0:T(8,128)} fusion(s32[2048]{0:T(1024)S(1)} %reshape.98, f32[]{:T(128)} %constant.15.clone.1, f32[256,256]{1,0:T(8,128)S(1)} %broadcast_multiply_fusion), kind=kCustom, calls=%fused_computation.10 | custom fusion | flops 524288 | bytes 4456452 | tf_op jit(solution)/shard_map/scatter-add | solution.py:81
  471.8 0.0 all-reduce.2.cloned.1.call-update
  471.9 0.2 reshape.90
  472.0 0.8 copy.46
  472.9 277.2 %all-reduce.2.cloned.1.call-done = f32[4096,256]{1,0:T(8,128)} async-done(((f32[4096,256]{1,0:T(8,128)}), f32[4096,256]{1,0:T(8,128)}) %all-reduce.2.cloned.1.call-update) | async-done | bytes 4194320 | tf_op jit(solution)/shard_map/psum | solution.py:82
  750.1 6.0 multiply_subtract_fusion
  756.1 0.0 all-to-all-done.3
  756.1 13.0 %scatter_custom_fusion = f32[2048,256]{1,0:T(8,128)} fusion(s32[2048]{0:T(1024)S(1)} %reshape.90, f32[256,1,1,8,256]{4,3,2,1,0:T(8,128)S(1)} %all-to-all-done.3, f32[]{:T(128)} %constant.15.clone.1), kind=kCustom, calls=%fused_computation.7 | custom fusion | flops 524288 | bytes 4194308 | tf_op jit(solution)/shard_map/scatter-add | solution.py:76
  769.2 0.0 copy-start
  769.2 3.9 scatter_custom_fusion.2
  773.0 0.0 copy-done
  773.0 3.2 multiply_subtract_fusion.1
  (6 shorter events, 0.0 us)
Async XLA Ops:
  7.2 425.0 %all-gather.3.cloned.1.call-start = ((), (), s32[]{:S(2)}) async-start(), calls=%async_computation.5 | async-start | bytes 4210688 | tf_op jit(solution)/shard_map/all_gather | solution.py:39
  7.9 0.5 copy-start.6
  12.7 27.0 %all-to-all-start = ((s32[256,1,1,8]{3,2,1,0:T(1,128)}), s32[256,1,1,8]{3,2,1,0:T(1,128)S(1)}, u32[]{:S(2)}, u32[]{:S(2)}) async-start(s32[256,1,1,8]{3,2,1,0:T(1,128)} %bitcast), calls=%async_computation | async-start | bytes 262144 | tf_op jit(solution)/shard_map/all_to_all | solution.py:25
  81.6 5.7 copy-start.1
  81.6 6.6 copy-start.2
  81.6 6.8 copy-start.4
  82.6 18.3 %all-to-all-start.2 = ((bf16[64,4,8,256]{3,2,0,1:T(8,128)(2,1)}), bf16[64,4,8,256]{3,2,0,1:T(8,128)(2,1)S(1)}, u32[]{:S(2)}, u32[]{:S(2)}) async-start(bf16[64,4,8,256]{3,2,0,1:T(8,128)(2,1)} %copy.39), calls=%async_computation.2 | async-start | bytes 2097152 | tf_op jit(solution)/shard_map/all_to_all | solution.py:44
  442.0 2.8 copy-start.5
  448.2 9.6 %copy-start.3 = (s32[256,8]{0,1:T(8,128)S(1)}, s32[256,8]{0,1:T(8,128)}, u32[]{:S(2)}) copy-start(s32[256,8]{0,1:T(8,128)} %param.11) | copy-start | bytes 24580
  448.2 308.0 %all-to-all-start.3 = ((f32[256,1,1,8,256]{4,3,2,1,0:T(8,128)}), f32[256,1,1,8,256]{4,3,2,1,0:T(8,128)S(1)}, u32[]{:S(2)}, u32[]{:S(2)}) async-start(f32[256,1,1,8,256]{4,3,2,1,0:T(8,128)} %fusion.7), calls=%async_computation.3 | async-start | bytes 4194304 | tf_op jit(solution)/shard_map/all_to_all | solution.py:25
  457.5 292.6 %all-reduce.2.cloned.1.call-start = ((), (), s32[]{:S(2)}) async-start(), calls=%async_computation.4 | async-start | bytes 8388608 | tf_op jit(solution)/shard_map/psum | solution.py:82
  769.2 3.9 copy-start
Sparse Core Ops, SparseCore 0:
  11.3 420.7 all-gather.2
  472.0 278.0 all-reduce.1
where the time goes:
time: 784 us; the launch traced here: 783 us
  waiting for transfers between devices  630 us (80%)
  other arithmetic  45.5 us (6%)
  blocking collectives  34.3 us (4%)
  starting transfers between devices  29 us (4%)
  local copies, waits for them, and re-layouts  24.8 us (3%)
  between operations  14.2 us (2%)
    all_gather x1, waiting for transfers between devices, body(): lax.all_gather(table[hot_slot], ('rows', 'grp'), axis=0, tiled=True)  330 us
    psum x1, waiting for transfers between devices, body(): summed = lax.psum(hot_local, ('rows', 'grp'))  277 us
    all_to_all x1, blocking collectives, body(): lax.all_to_all(looked, 'rows', split_axis=0, concat_axis=0, tiled=True)  34.3 us
    all_to_all x2, starting transfers between devices, exchange_both(): lax.all_to_all(blocks, axis, split_axis=0, concat_axis=0, tiled=True)  24 us
  transfers between devices with their start and end apart: 5, of which 4 were waited for; matrix products, arithmetic and copies ran while one was open for 5% of the time, Pallas kernels for 0%

commit v1 on v0

--- a/solution.py
+++ b/solution.py
@@ -2,6 +2,7 @@
 import jax.numpy as jnp
 from jax import lax
 from jax.sharding import PartitionSpec as P
+from jax.lax import all_to_all, axis_size
 
 
 def split_up(value, dim, peers):
@@ -36,7 +37,12 @@
     slots = cold_row.shape[1] * cold_row.shape[2]
     per_peer = cold_row.shape[2]
     rounded = table.astype(jnp.bfloat16)
-    hot_full = lax.all_gather(table[hot_slot], ("rows", "grp"), axis=0, tiled=True)
+    hot_full = jnp.concatenate(
+        all_to_all(
+            jnp.stack([table[hot_slot]] * axis_size(("rows", "grp"))), ("rows", "grp"), 0, 0
+        ),
+        0,
+    )
     hot_copy = hot_full.astype(jnp.bfloat16)
     requests = cold_row[0].reshape(n_rows, n_grp, per_peer)
     arrived = exchange_both(requests, ("rows", "grp"), ("rows", "grp"), (0, 1), (0, 1))

time: 784 us -> 554 us (0.71)
  waiting for transfers between devices: 630 us -> 391 us
  starting transfers between devices: 29 us -> 36.9 us
    all_gather x1 -> x0, waiting for transfers between devices: 330 us -> none  [body(): lax.all_gather(table[hot_slot], ('rows', 'grp'), axis=0, tiled=True)]
    all_to_all x0 -> x1, waiting for transfers between devices: none -> 93 us  [body(): all_to_all(jnp.stack([table[hot_slot]] * axis_size(('rows', 'grp'))), ('r...]
    all_to_all x0 -> x1, starting transfers between devices: none -> 9.22 us  [body(): all_to_all(jnp.stack([table[hot_slot]] * axis_size(('rows', 'grp'))), ('r...]
where the time goes in v1:
time: 554 us; the launch traced here: 553 us
  waiting for transfers between devices  391 us (71%)
  other arithmetic  44.8 us (8%)
  starting transfers between devices  36.9 us (7%)
  blocking collectives  34.3 us (6%)
  local copies, waits for them, and re-layouts  26.7 us (5%)
  between operations  14.2 us (3%)
    psum x1, waiting for transfers between devices, body(): summed = lax.psum(hot_local, ('rows', 'grp'))  277 us
    all_to_all x1, waiting for transfers between devices, body(): all_to_all(jnp.stack([table[hot_slot]] * axis_size(('rows', 'grp'))), ('r...  93 us
    all_to_all x1, blocking collectives, body(): lax.all_to_all(looked, 'rows', split_axis=0, concat_axis=0, tiled=True)  34.3 us
    all_to_all x2, starting transfers between devices, exchange_both(): lax.all_to_all(blocks, axis, split_axis=0, concat_axis=0, tiled=True)  22.7 us
    scatter-add x1, other arithmetic, body(): jax.ops.segment_sum(spread, hot_pick.reshape(-1), num_segments=hot_total)  13.8 us
    scatter-add x1, other arithmetic, body(): jax.ops.segment_sum(delivered.reshape(slots, width), arrived.reshape(slot...  13 us
  transfers between devices with their start and end apart: 5, of which 4 were waited for; matrix products, arithmetic and copies ran while one was open for 5% of the time, Pallas kernels for 0%

profile of v1, /device:TPU:2, one launch (start us, length us, event | category | flops | bytes accessed | tf_op | source)
XLA Modules:
  0.0 553.0 jit_solution(8040631235972596761)
XLA Ops:
  7.2 1.5 copy.38
  8.7 14.7 %all-to-all-start = ((s32[256,1,1,8]{3,2,1,0:T(1,128)}), s32[256,1,1,8]{3,2,1,0:T(1,128)S(1)}, u32[]{:S(2)}, u32[]{:S(2)}) async-start(s32[256,1,1,8]{3,2,1,0:T(1,128)} %bitcast), calls=%async_computation | async-start | bytes 262144 | tf_op jit(solution)/shard_map/all_to_all | solution.py:26
  23.3 1.7 convert_element_type.14
  25.0 10.6 %all-to-all-done = s32[256,1,1,8]{3,2,1,0:T(1,128)S(1)} async-done(((s32[256,1,1,8]{3,2,1,0:T(1,128)}), s32[256,1,1,8]{3,2,1,0:T(1,128)S(1)}, u32[]{:S(2)}, u32[]{:S(2)}) %all-to-all-start) | async-done | bytes 8224 | tf_op jit(solution)/shard_map/all_to_all | solution.py:26
  35.6 0.2 reshape_reshape.6
  35.8 7.5 %gather_fusion = bf16[2048,256]{1,0:T(8,128)(2,1)S(1)} fusion(bf16[2048,256]{1,0:T(8,128)(2,1)S(1)} %convert_element_type.14, s32[2048]{0:T(1024)S(1)} %broadcast_clamp_fusion.1), kind=kCustom, calls=%fused_computation | custom fusion | bytes 2105344 | tf_op jit(solution)/shard_map/gather | solution.py:49
  43.3 34.3 %all_to_all.25 = bf16[64,4,8,256]{3,2,1,0:T(8,128)(2,1)S(1)} all-to-all(bf16[64,4,8,256]{3,2,1,0:T(8,128)(2,1)S(1)} %bitcast.41), channel_id=1, replica_groups=mesh['rows'=64,'grp'=4] {'rows'}, dimensions={0} | all-to-all | bytes 2097152 | tf_op jit(solution)/shard_map/all_to_all | solution.py:51
  77.6 0.0 copy-start.7
  77.6 1.0 copy.39
  78.6 4.7 all-to-all-start.2
  83.3 0.0 copy-done.7
  83.3 0.0 copy-start.6
  83.3 0.5 copy-done.6
  83.9 2.2 gather_fusion.1
  86.0 10.1 %all-to-all-done.2 = bf16[64,4,8,256]{3,2,0,1:T(8,128)(2,1)S(1)} async-done(((bf16[64,4,8,256]{3,2,0,1:T(8,128)(2,1)}), bf16[64,4,8,256]{3,2,0,1:T(8,128)(2,1)S(1)}, u32[]{:S(2)}, u32[]{:S(2)}) %all-to-all-start.2) | async-done | bytes 1048608 | tf_op jit(solution)/shard_map/all_to_all | solution.py:50
  96.1 2.5 stack.2
  98.7 0.0 copy-start.1
  98.7 0.0 copy-start.2
  98.7 0.0 copy-start.4
  98.7 9.2 %all-to-all-start.3 = ((f32[256,16,256]{2,1,0:T(8,128)}), f32[256,16,256]{2,1,0:T(8,128)}, u32[]{:S(2)}, u32[]{:S(2)}) async-start(f32[256,16,256]{2,1,0:T(8,128)} %stack.2), calls=%async_computation.3 | async-start | bytes 8388608 | tf_op jit(solution)/shard_map/all_to_all | solution.py:41
  107.9 0.0 copy-done.1
  107.9 0.8 copy.43
  108.7 0.0 copy-done.2
  108.7 0.1 copy.41
  108.9 0.1 reshape.88
  109.0 0.0 copy-done.4
  109.0 0.1 copy.37
  109.1 0.1 eq.16
  109.3 1.1 copy.40
  110.4 93.0 %all-to-all-done.3 = f32[256,16,256]{2,1,0:T(8,128)} async-done(((f32[256,16,256]{2,1,0:T(8,128)}), f32[256,16,256]{2,1,0:T(8,128)}, u32[]{:S(2)}, u32[]{:S(2)}) %all-to-all-start.3) | async-done | bytes 4194336 | tf_op jit(solution)/shard_map/all_to_all | solution.py:41
  203.4 2.4 bitcast_convert_fusion
  205.8 7.5 %gather_fusion.2 = bf16[2048,256]{1,0:T(8,128)(2,1)S(1)} fusion(bf16[4096,256]{1,0:T(8,128)(2,1)S(1)} %bitcast_convert_fusion, s32[2048]{0:T(1024)S(1)} %broadcast_clamp_fusion), kind=kCustom, calls=%fused_computation.2 | custom fusion | bytes 2105344 | tf_op jit(solution)/shard_map/gather | solution.py:63
  213.3 0.0 copy-start.5
  213.3 0.7 convert_reduce_fusion
  214.0 0.1 copy.42
  214.1 2.0 multiply_reduce_fusion
  216.1 0.0 copy-done.5
  216.1 0.1 broadcast_multiply_fusion
  216.3 3.2 fusion.7
  219.4 0.0 copy-start.3
  219.4 8.1 %all-to-all-start.4 = ((f32[256,1,1,8,256]{4,3,2,1,0:T(8,128)}), f32[256,1,1,8,256]{4,3,2,1,0:T(8,128)S(1)}, u32[]{:S(2)}, u32[]{:S(2)}) async-start(f32[256,1,1,8,256]{4,3,2,1,0:T(8,128)} %fusion.7), calls=%async_computation.4 | async-start | bytes 4194304 | tf_op jit(solution)/shard_map/all_to_all | solution.py:26
  227.5 0.2 all-reduce.2.cloned.1.call-start
  227.7 0.0 copy-done.3
  227.7 0.1 copy.45
  227.8 0.1 reshape.104
  228.0 13.8 %scatter_custom_fusion.1 = f32[4096,256]{1,0:T(8,128)} fusion(s32[2048]{0:T(1024)S(1)} %reshape.104, f32[]{:T(128)} %constant.15.clone.1, f32[256,256]{1,0:T(8,128)S(1)} %broadcast_multiply_fusion), kind=kCustom, calls=%fused_computation.11 | custom fusion | flops 524288 | bytes 4456452 | tf_op jit(solution)/shard_map/scatter-add | solution.py:87
  241.8 0.0 all-reduce.2.cloned.1.call-update
  241.8 0.2 reshape.96
  242.0 0.8 copy.46
  242.8 277.2 %all-reduce.2.cloned.1.call-done = f32[4096,256]{1,0:T(8,128)} async-done(((f32[4096,256]{1,0:T(8,128)}), f32[4096,256]{1,0:T(8,128)}) %all-reduce.2.cloned.1.call-update) | async-done | bytes 4194320 | tf_op jit(solution)/shard_map/psum | solution.py:88
  520.1 6.0 %bitcast_subtract_fusion = f32[4096,256]{1,0:T(8,128)} fusion(f32[256,16,256]{2,1,0:T(8,128)} %all-to-all-done.3, f32[4096,256]{1,0:T(8,128)} %all-reduce.2.cloned.1.call-done), kind=kLoop, calls=%fused_computation.6 | loop fusion | flops 2097152 | bytes 12582912 | tf_op jit(solution)/shard_map/sub | solution.py:93
  526.1 0.0 all-to-all-done.4
  526.1 13.0 %scatter_custom_fusion = f32[2048,256]{1,0:T(8,128)} fusion(s32[2048]{0:T(1024)S(1)} %reshape.96, f32[256,1,1,8,256]{4,3,2,1,0:T(8,128)S(1)} %all-to-all-done.4, f32[]{:T(128)} %constant.15.clone.1), kind=kCustom, calls=%fused_computation.8 | custom fusion | flops 524288 | bytes 4194308 | tf_op jit(solution)/shard_map/scatter-add | solution.py:82
  539.1 0.0 copy-start
  539.1 3.9 scatter_custom_fusion.2
  543.0 0.0 copy-done
  543.0 3.2 multiply_subtract_fusion
  (7 shorter events, 0.0 us)
Async XLA Ops:
  8.7 27.0 %all-to-all-start = ((s32[256,1,1,8]{3,2,1,0:T(1,128)}), s32[256,1,1,8]{3,2,1,0:T(1,128)S(1)}, u32[]{:S(2)}, u32[]{:S(2)}) async-start(s32[256,1,1,8]{3,2,1,0:T(1,128)} %bitcast), calls=%async_computation | async-start | bytes 262144 | tf_op jit(solution)/shard_map/all_to_all | solution.py:26
  77.6 5.7 %copy-start.7 = (s32[16]{0:T(128)S(1)}, s32[16]{0:T(128)}, u32[]{:S(2)}) copy-start(s32[16]{0:T(128)} %param.8) | copy-start | bytes 196
  78.6 17.5 %all-to-all-start.2 = ((bf16[64,4,8,256]{3,2,0,1:T(8,128)(2,1)}), bf16[64,4,8,256]{3,2,0,1:T(8,128)(2,1)S(1)}, u32[]{:S(2)}, u32[]{:S(2)}) async-start(bf16[64,4,8,256]{3,2,0,1:T(8,128)(2,1)} %copy.39), calls=%async_computation.2 | async-start | bytes 2097152 | tf_op jit(solution)/shard_map/all_to_all | solution.py:50
  83.3 0.5 copy-start.6
  98.7 9.2 %copy-start.1 = (f32[256,256]{1,0:T(8,128)S(1)}, f32[256,256]{1,0:T(8,128)}, u32[]{:S(2)}) copy-start(f32[256,256]{1,0:T(8,128)} %param.12) | copy-start | bytes 786436
  98.7 10.1 %copy-start.2 = (s32[256,8]{0,1:T(8,128)S(1)}, s32[256,8]{0,1:T(8,128)}, u32[]{:S(2)}) copy-start(s32[256,8]{0,1:T(8,128)} %param.11) | copy-start | bytes 24580
  98.7 10.3 %copy-start.4 = (s32[1,256,8]{1,2,0:T(8,128)S(1)}, s32[1,256,8]{1,2,0:T(8,128)}, u32[]{:S(2)}) copy-start(s32[1,256,8]{1,2,0:T(8,128)} %param.10) | copy-start | bytes 24580
  98.7 104.7 %all-to-all-start.3 = ((f32[256,16,256]{2,1,0:T(8,128)}), f32[256,16,256]{2,1,0:T(8,128)}, u32[]{:S(2)}, u32[]{:S(2)}) async-start(f32[256,16,256]{2,1,0:T(8,128)} %stack.2), calls=%async_computation.3 | async-start | bytes 8388608 | tf_op jit(solution)/shard_map/all_to_all | solution.py:41
  213.3 2.8 copy-start.5
  219.4 8.3 %copy-start.3 = (s32[256,8]{0,1:T(8,128)S(1)}, s32[256,8]{0,1:T(8,128)}, u32[]{:S(2)}) copy-start(s32[256,8]{0,1:T(8,128)} %param.11) | copy-start | bytes 24580
  219.4 306.7 %all-to-all-start.4 = ((f32[256,1,1,8,256]{4,3,2,1,0:T(8,128)}), f32[256,1,1,8,256]{4,3,2,1,0:T(8,128)S(1)}, u32[]{:S(2)}, u32[]{:S(2)}) async-start(f32[256,1,1,8,256]{4,3,2,1,0:T(8,128)} %fusion.7), calls=%async_computation.4 | async-start | bytes 4194304 | tf_op jit(solution)/shard_map/all_to_all | solution.py:26
  227.5 292.6 %all-reduce.2.cloned.1.call-start = ((), (), s32[]{:S(2)}) async-start(), calls=%async_computation.5 | async-start | bytes 8388608 | tf_op jit(solution)/shard_map/psum | solution.py:88
  539.1 3.9 copy-start
Sparse Core Ops, SparseCore 0:
  242.0 278.0 all-reduce.1
